TPU v7x, 512 devices: a whole 4x4x16 slice. The times are simulated.
512 devices in a mesh: probe: 16 (over y, x), space: 32 (over z, core).
Axes of the slice: x: 4, y: 4, z: 16, core: 2. Of those that a mesh axis runs over, the one named last changes fastest.
Arguments:
- probes: float32 [128, 131072], P('probe', 'space'), may hold values from -6 to 6
- sensitivity: float32 [8, 8, 65536], P(None, None, 'space'), may hold values from -2.1 to 2.1
- obs_weight: float32 [8, 65536], P(None, 'space'), may hold values from 0.5 to 4
- prior_weight: float32 [131072], P('space'), may hold values from 0.2 to 2
- connectivity: int32 [8, 65536], P(None, 'space'), may hold values from 0 to 4351, as said below
Outputs:
- basis: float32 [128, 131072], P('probe', 'space')
- factor: float32 [128, 128], replicated
Inputs may be any that keep to these rules, and one draw needn't show every extreme that they name: Each column holds 8 distinct numbers. For an element of the block of device d of space (columns d * 2048 to (d + 1) * 2048 - 1), connectivity + d * 4096 - 128 is an existing node, and the values 0 and 4351 are both named wherever those nodes exist.
All inputs are finite; a program needn't handle non-finite values.
Results may differ from a plain program's by a relative error of at most 0.0003.
Values sent between devices are 32-bit elements; how exact they have to be, the bound alone decides.
No kernel may reach another device: no remote copies, remote signals or barrier semaphores. Data moves between devices by JAX's collectives and lax.ppermute only.
A program may use at most 64 MiB of HBM per device.

v0:
```python
import math
import jax
import jax.numpy as jnp
from jax import lax
from jax.sharding import PartitionSpec as P

HALO = 128
highest = lax.Precision.HIGHEST


def extended_2(block, sides, width):
    for axis, dim in sides:
        count = lax.axis_size(axis)
        forward = [(i, i + 1) for i in range(count - 1)]
        backward = [(target, source) for source, target in forward]
        low = lax.ppermute(
            lax.slice_in_dim(block, block.shape[dim] - width, None, axis=dim), axis, forward
        )
        high = lax.ppermute(lax.slice_in_dim(block, 0, width, axis=dim), axis, backward)
        block = jnp.concatenate([low, block, high], axis=dim)
    return block


def shifted(block, axis, distance):
    devices = range(lax.axis_size(axis))
    route = [(i - distance, i) for i in devices if i - distance in devices]
    return lax.ppermute(block, axis, route)


def element_images(extended, sensitivity, obs_weight, local):
    gathered = extended[:, local]
    gauss_count = sensitivity.shape[0]
    corner_count = sensitivity.shape[1]
    observed = []
    for gauss in range(gauss_count):
        total = gathered[:, 0, :] * sensitivity[gauss, 0][None, :]
        for corner in range(1, corner_count):
            total = total + gathered[:, corner, :] * sensitivity[gauss, corner][None, :]
        observed.append(total * obs_weight[gauss][None, :])
    pulled = []
    for corner in range(corner_count):
        total = observed[0] * sensitivity[0, corner][None, :]
        for gauss in range(1, gauss_count):
            total = total + observed[gauss] * sensitivity[gauss, corner][None, :]
        pulled.append(total)
    pulled = jnp.stack(pulled, axis=1)
    return jnp.zeros(extended.shape, jnp.float32).at[:, local].add(pulled)


def gram_over_space(partial_value):
    return lax.psum(partial_value, "space")


def orthonormal(rows, reduce_gram):
    gram_first = reduce_gram(
        jnp.dot(rows, rows.T, precision=highest, preferred_element_type=jnp.float32)
    )
    lower_first = jnp.linalg.cholesky(gram_first)
    basis_first = lax.linalg.triangular_solve(lower_first, rows, left_side=True, lower=True)
    gram_second = reduce_gram(
        jnp.dot(basis_first, basis_first.T, precision=highest, preferred_element_type=jnp.float32)
    )
    lower_second = jnp.linalg.cholesky(gram_second)
    basis = lax.linalg.triangular_solve(lower_second, basis_first, left_side=True, lower=True)
    factor = jnp.dot(
        lower_first, lower_second, precision=highest, preferred_element_type=jnp.float32
    ).T
    return (basis, factor)


def on_device(probes, sensitivity, obs_weight, prior_weight, connectivity):
    node_count = probes.shape[1]
    probe_count = probes.shape[0]
    extended = extended_2(probes, (("space", 1),), HALO)
    summed = element_images(extended, sensitivity, obs_weight, connectivity)
    lower_rim = shifted(summed[:, :HALO], "space", -1)
    upper_rim = shifted(summed[:, HALO + node_count :], "space", 1)
    images = summed[:, HALO : HALO + node_count] + prior_weight[None, :] * probes
    images = images.at[:, node_count - HALO :].add(lower_rim)
    images = images.at[:, :HALO].add(upper_rim)
    scale = math.sqrt(float(node_count * lax.axis_size("space")))
    whole = lax.all_gather(images, "probe", axis=0, tiled=True)
    basis, factor = orthonormal(whole, gram_over_space)
    basis = lax.dynamic_slice_in_dim(basis, lax.axis_index("probe") * probe_count, probe_count, 0)
    return (basis * scale, factor / scale)


def solution(mesh):
    return jax.shard_map(
        on_device,
        mesh=mesh,
        in_specs=(
            P("probe", "space"),
            P(None, None, "space"),
            P(None, "space"),
            P("space"),
            P(None, "space"),
        ),
        out_specs=(P("probe", "space"), P()),
        check_vma=False,
    )
```

profile of v0, /device:TPU:1, one launch (start us, length us, event | category | flops | bytes accessed | tf_op | source)
XLA Modules:
  0.0 697.5 jit_solution(16327532529719816883)
XLA Ops:
  7.9 4.9 collective-permute-start
  12.8 5.1 collective-permute-start.1
  18.0 1.7 fusion.28
  19.7 1.7 fusion.27
  21.4 1.9 fusion.26
  28.8 54.8 %gather_fusion = f32[16384,8]{1,0:T(8,128)} fusion(f32[8,4352]{0,1:T(8,128)S(1)} %copy.43, s32[16384]{0:T(1024)S(1)} %broadcast_clamp_fusion), kind=kCustom, calls=%fused_computation | custom fusion | bytes 1114112 | tf_op jit(solution)/shard_map/gather | solution.py:31
  83.6 5.5 copy.44
  91.7 4.6 copy.63
  96.3 88.2 %scatter_custom_fusion = f32[8,4352]{0,1:T(8,128)S(1)} fusion(s32[16384]{0:T(1024)S(1)} %bitcast.108, f32[16384,8]{1,0:T(8,128)} %bitcast.104, f32[]{:T(128)} %constant.95.clone.1), kind=kCustom, calls=%fused_computation.3 | custom fusion | flops 131072 | bytes 139776 | tf_op jit(solution)/shard_map/scatter-add | solution.py:47
  185.9 2.2 copy.64
  188.2 1.9 collective-permute-start.2
  190.2 3.7 collective-permute-start.3
  195.9 62.5 %all-gather.2.cloned.1.call-done = f32[128,4096]{1,0:T(8,128)} async-done(((f32[8,4096]{1,0:T(8,128)}), f32[128,4096]{1,0:T(8,128)}) %all-gather.2.cloned.1.call-update) | async-done | bytes 2097168 | tf_op jit(solution)/shard_map/all_gather | solution.py:82
  258.5 4.7 fusion.32
  263.4 187.4 %all-reduce.3.cloned.1.call-done = f32[128,128]{0,1:T(8,128)} async-done(((f32[128,128]{0,1:T(8,128)}), f32[128,128]{0,1:T(8,128)}) %all-reduce.3.cloned.1.call-update) | async-done | bytes 65552 | tf_op jit(solution)/shard_map/psum | solution.py:51
  452.6 11.7 %cholesky.44 = f32[128,128]{1,0:T(8,128)S(1)} custom-call(f32[128,128]{1,0:T(8,128)S(1)} %fusion.8), custom_call_target="Cholesky" | custom-call | tf_op jit(solution)/shard_map/jit(cholesky)/cholesky | solution.py:58
  465.7 9.8 %custom-call.6 = f32[1,128,128]{1,2,0:T(8,128)S(1)} custom-call(f32[1,128,128]{2,1,0:T(8,128)S(1)} %fusion.12), custom_call_target="InvertDiagBlocksLowerTriangular" | custom-call | tf_op jit(solution)/shard_map/triangular_solve/custom-call.0 | solution.py:59
  475.5 3.5 fusion.6
  479.0 2.4 fusion.33
  481.5 179.9 %all-reduce.5.cloned.1.call-done = f32[128,128]{0,1:T(8,128)} async-done(((f32[128,128]{0,1:T(8,128)}), f32[128,128]{0,1:T(8,128)}) %all-reduce.5.cloned.1.call-update) | async-done | bytes 65552 | tf_op jit(solution)/shard_map/psum | solution.py:51
  663.2 11.9 %cholesky.55 = f32[128,128]{1,0:T(8,128)S(1)} custom-call(f32[128,128]{1,0:T(8,128)S(1)} %fusion.5), custom_call_target="Cholesky" | custom-call | tf_op jit(solution)/shard_map/jit(cholesky)/cholesky | solution.py:63
  675.8 2.1 convolution_multiply_fusion
  678.5 9.8 %custom-call.7 = f32[1,128,128]{1,2,0:T(8,128)S(1)} custom-call(f32[1,128,128]{2,1,0:T(8,128)S(1)} %select_bitcast_fusion), custom_call_target="InvertDiagBlocksLowerTriangular" | custom-call | tf_op jit(solution)/shard_map/triangular_solve/custom-call.0 | solution.py:64
  688.3 1.9 fusion.3
  (60 shorter events, 19.5 us)
Async XLA Ops:
  7.2 251.3 %all-gather.2.cloned.1.call-start = ((), (), s32[]{:S(2)}) async-start(), calls=%async_computation | async-start | bytes 2228224 | tf_op jit(solution)/shard_map/all_gather | solution.py:82
  7.9 19.3 %collective-permute-start = (f32[8,128]{1,0:T(8,128)S(1)}, f32[8,128]{1,0:T(8,128)S(1)}, u32[]{:S(2)}, u32[]{:S(2)}) collective-permute-start(f32[8,128]{1,0:T(8,128)S(1)} %get-tuple-element.103), channel_id=1, source_target_pairs={{0,1},{1,2},{2,3},{3,4},{4,5},{5,6},{6,7},{7,8},{8,9},{9,10},{10,1... | collective-permute-start | bytes 12296 | tf_op jit(solution)/shard_map/ppermute | solution.py:16
  12.8 14.4 %collective-permute-start.1 = (f32[8,128]{1,0:T(8,128)S(1)}, f32[8,128]{1,0:T(8,128)S(1)}, u32[]{:S(2)}, u32[]{:S(2)}) collective-permute-start(f32[8,128]{1,0:T(8,128)S(1)} %get-tuple-element.104), channel_id=1, source_target_pairs={{1,0},{2,1},{3,2},{4,3},{5,4},{6,5},{7,6},{8,7},{9,8},{10,9},{11,1... | collective-permute-start | bytes 12296 | tf_op jit(solution)/shard_map/ppermute | solution.py:19
  185.9 7.9 %copy-start = (f32[8,4096]{1,0:T(8,128)S(1)}, f32[8,4096]{1,0:T(8,128)}, u32[]{:S(2)}) copy-start(f32[8,4096]{1,0:T(8,128)} %param.12) | copy-start | bytes 393220
  185.9 7.9 %copy-start.2 = (f32[4096]{0:T(1024)S(1)}, f32[4096]{0:T(1024)}, u32[]{:S(2)}) copy-start(f32[4096]{0:T(1024)} %param.15) | copy-start | bytes 49156
  188.2 5.7 collective-permute-start.2
  190.2 4.4 collective-permute-start.3
  195.2 0.7 copy-start.1
  195.9 255.0 %all-reduce.3.cloned.1.call-start = ((), (), s32[]{:S(2)}) async-start(), calls=%async_computation.1 | async-start | bytes 131072 | tf_op jit(solution)/shard_map/psum | solution.py:51
  263.2 398.2 %all-reduce.5.cloned.1.call-start = ((), (), s32[]{:S(2)}) async-start(), calls=%async_computation.2 | async-start | bytes 131072 | tf_op jit(solution)/shard_map/psum | solution.py:51
Sparse Core Ops, SparseCore 0:
  196.0 62.4 all-gather.1
  263.3 187.4 all-reduce.2
  481.6 179.7 all-reduce.4
where the time goes:
time: 698 us; the launch traced here: 697 us
  waiting for transfers between devices  431 us (62%)
  other arithmetic  141 us (20%)
  local copies, waits for them, and re-layouts  81.6 us (12%)
  starting transfers between devices  15.9 us (2%)
  matrix products  14.7 us (2%)
  between operations  14.1 us (2%)
    psum x2, waiting for transfers between devices, gram_over_space(): return lax.psum(partial_value, 'space')  367 us
    scatter-add x1, other arithmetic, element_images(): return jnp.zeros(extended.shape, jnp.float32).at[:, local].add(pulled)  88.2 us
    all_gather x1, waiting for transfers between devices, on_device(): whole = lax.all_gather(images, 'probe', axis=0, tiled=True)  62.5 us
    gather x2, local copies, waits for them, and re-layouts, element_images(): gathered = extended[:, local]  60.3 us
  transfers between devices with their start and end apart: 7, of which 4 were waited for; matrix products, arithmetic and copies ran while one was open for 1% of the time, Pallas kernels for 0%

commit v1 on v0

--- a/solution.py
+++ b/solution.py
@@ -79,7 +79,10 @@
     images = images.at[:, node_count - HALO :].add(lower_rim)
     images = images.at[:, :HALO].add(upper_rim)
     scale = math.sqrt(float(node_count * lax.axis_size("space")))
-    whole = lax.all_gather(images, "probe", axis=0, tiled=True)
+    size = lax.axis_size("probe")
+    blocks = jnp.stack([images for _ in range(size)])
+    blocks = lax.all_to_all(blocks, "probe", split_axis=0, concat_axis=0)
+    whole = jnp.concatenate(blocks, axis=0)
     basis, factor = orthonormal(whole, gram_over_space)
     basis = lax.dynamic_slice_in_dim(basis, lax.axis_index("probe") * probe_count, probe_count, 0)
     return (basis * scale, factor / scale)

time: 698 us -> 667 us (0.956)
  waiting for transfers between devices: 431 us -> 368 us
  blocking collectives: 0 us -> 31.7 us
    all_gather x1 -> x0, waiting for transfers between devices: 62.5 us -> none  [on_device(): whole = lax.all_gather(images, 'probe', axis=0, tiled=True)]
    all_to_all x0 -> x1, blocking collectives: none -> 31.7 us  [on_device(): blocks = lax.all_to_all(blocks, 'probe', split_axis=0, concat_axis=0)]
  transfers between devices with their start and end apart: 7 -> 6, of which waited for: 4 -> 3; matrix products, arithmetic and copies ran while one was open for 1% -> 1% of each run, Pallas kernels for 0% -> 0%
where the time goes in v1:
time: 667 us; the launch traced here: 666 us
  waiting for transfers between devices  368 us (55%)
  other arithmetic  141 us (21%)
  local copies, waits for them, and re-layouts  82.2 us (12%)
  blocking collectives  31.7 us (5%)
  starting transfers between devices  15.9 us (2%)
  between operations  14.4 us (2%)
  matrix products  12.5 us (2%)
    psum x2, waiting for transfers between devices, gram_over_space(): return lax.psum(partial_value, 'space')  367 us
    scatter-add x1, other arithmetic, element_images(): return jnp.zeros(extended.shape, jnp.float32).at[:, local].add(pulled)  88.2 us
    gather x2, local copies, waits for them, and re-layouts, element_images(): gathered = extended[:, local]  60 us
    all_to_all x1, blocking collectives, on_device(): blocks = lax.all_to_all(blocks, 'probe', split_axis=0, concat_axis=0)  31.7 us
  transfers between devices with their start and end apart: 6, of which 3 were waited for; matrix products, arithmetic and copies ran while one was open for 1% of the time, Pallas kernels for 0%

profile of v1, /device:TPU:1, one launch (start us, length us, event | category | flops | bytes accessed | tf_op | source)
XLA Modules:
  0.0 665.6 jit_solution(11118709685910277258)
XLA Ops:
  7.9 4.9 collective-permute-start
  12.8 5.1 collective-permute-start.1
  18.0 1.7 fusion.31
  19.7 1.7 fusion.30
  21.4 1.9 fusion.29
  28.8 54.4 %gather_fusion = f32[16384,8]{1,0:T(8,128)} fusion(f32[8,4352]{0,1:T(8,128)S(1)} %copy.44, s32[16384]{0:T(1024)S(1)} %broadcast_clamp_fusion), kind=kCustom, calls=%fused_computation | custom fusion | bytes 1114112 | tf_op jit(solution)/shard_map/gather | solution.py:31
  83.2 5.5 copy.45
  91.4 4.5 copy.64
  95.9 88.2 %scatter_custom_fusion = f32[8,4352]{0,1:T(8,128)S(1)} fusion(s32[16384]{0:T(1024)S(1)} %bitcast.110, f32[16384,8]{1,0:T(8,128)} %bitcast.106, f32[]{:T(128)} %constant.97.clone.1), kind=kCustom, calls=%fused_computation.7 | custom fusion | flops 131072 | bytes 139776 | tf_op jit(solution)/shard_map/scatter-add | solution.py:47
  185.6 2.2 copy.65
  187.8 1.9 collective-permute-start.2
  189.8 3.7 collective-permute-start.3
  195.1 31.7 %all_to_all.5 = f32[16,8,4096]{2,1,0:T(8,128)S(1)} all-to-all(f32[16,8,4096]{2,1,0:T(8,128)S(1)} %stack.5), channel_id=1, replica_groups=mesh['probe'=16,'space'=32] {'probe'}, dimensions={0} | all-to-all | bytes 4194304 | tf_op jit(solution)/shard_map/all_to_all | solution.py:84
  228.2 2.4 fusion.2
  230.9 187.5 %all-reduce.3.cloned.1.call-done = f32[128,128]{0,1:T(8,128)} async-done(((f32[128,128]{0,1:T(8,128)}), f32[128,128]{0,1:T(8,128)}) %all-reduce.3.cloned.1.call-update) | async-done | bytes 65552 | tf_op jit(solution)/shard_map/psum | solution.py:51
  420.2 11.7 %cholesky.44 = f32[128,128]{1,0:T(8,128)S(1)} custom-call(f32[128,128]{1,0:T(8,128)S(1)} %fusion.11), custom_call_target="Cholesky" | custom-call | tf_op jit(solution)/shard_map/jit(cholesky)/cholesky | solution.py:58
  433.2 9.8 %custom-call.6 = f32[1,128,128]{1,2,0:T(8,128)S(1)} custom-call(f32[1,128,128]{2,1,0:T(8,128)S(1)} %fusion.15), custom_call_target="InvertDiagBlocksLowerTriangular" | custom-call | tf_op jit(solution)/shard_map/triangular_solve/custom-call.0 | solution.py:59
  443.0 3.5 fusion
  446.5 2.4 fusion.35
  449.0 179.9 %all-reduce.5.cloned.1.call-done = f32[128,128]{0,1:T(8,128)} async-done(((f32[128,128]{0,1:T(8,128)}), f32[128,128]{0,1:T(8,128)}) %all-reduce.5.cloned.1.call-update) | async-done | bytes 65552 | tf_op jit(solution)/shard_map/psum | solution.py:51
  630.7 11.9 %cholesky.55 = f32[128,128]{1,0:T(8,128)S(1)} custom-call(f32[128,128]{1,0:T(8,128)S(1)} %fusion.9), custom_call_target="Cholesky" | custom-call | tf_op jit(solution)/shard_map/jit(cholesky)/cholesky | solution.py:63
  643.4 2.3 convolution_multiply_fusion
  646.3 9.8 %custom-call.7 = f32[1,128,128]{1,2,0:T(8,128)S(1)} custom-call(f32[1,128,128]{2,1,0:T(8,128)S(1)} %select_bitcast_fusion), custom_call_target="InvertDiagBlocksLowerTriangular" | custom-call | tf_op jit(solution)/shard_map/triangular_solve/custom-call.0 | solution.py:64
  656.2 1.9 fusion.7
  (59 shorter events, 20.5 us)
Async XLA Ops:
  7.2 411.2 %all-reduce.3.cloned.1.call-start = ((), (), s32[]{:S(2)}) async-start(), calls=%async_computation.1 | async-start | bytes 131072 | tf_op jit(solution)/shard_map/psum | solution.py:51
  7.9 19.3 %collective-permute-start = (f32[8,128]{1,0:T(8,128)S(1)}, f32[8,128]{1,0:T(8,128)S(1)}, u32[]{:S(2)}, u32[]{:S(2)}) collective-permute-start(f32[8,128]{1,0:T(8,128)S(1)} %get-tuple-element.103), channel_id=1, source_target_pairs={{0,1},{1,2},{2,3},{3,4},{4,5},{5,6},{6,7},{7,8},{8,9},{9,10},{10,1... | collective-permute-start | bytes 12296 | tf_op jit(solution)/shard_map/ppermute | solution.py:16
  12.8 14.4 %collective-permute-start.1 = (f32[8,128]{1,0:T(8,128)S(1)}, f32[8,128]{1,0:T(8,128)S(1)}, u32[]{:S(2)}, u32[]{:S(2)}) collective-permute-start(f32[8,128]{1,0:T(8,128)S(1)} %get-tuple-element.104), channel_id=1, source_target_pairs={{1,0},{2,1},{3,2},{4,3},{5,4},{6,5},{7,6},{8,7},{9,8},{10,9},{11,1... | collective-permute-start | bytes 12296 | tf_op jit(solution)/shard_map/ppermute | solution.py:19
  185.6 7.9 %copy-start.1 = (f32[8,4096]{1,0:T(8,128)S(1)}, f32[8,4096]{1,0:T(8,128)}, u32[]{:S(2)}) copy-start(f32[8,4096]{1,0:T(8,128)} %param.12) | copy-start | bytes 393220
  185.6 7.9 %copy-start.2 = (f32[4096]{0:T(1024)S(1)}, f32[4096]{0:T(1024)}, u32[]{:S(2)}) copy-start(f32[4096]{0:T(1024)} %param.15) | copy-start | bytes 49156
  187.8 5.7 collective-permute-start.2
  189.8 4.4 collective-permute-start.3
  226.8 1.4 copy-start
  230.6 398.3 %all-reduce.5.cloned.1.call-start = ((), (), s32[]{:S(2)}) async-start(), calls=%async_computation.2 | async-start | bytes 131072 | tf_op jit(solution)/shard_map/psum | solution.py:51
Sparse Core Ops, SparseCore 0:
  230.8 187.5 all-reduce.2
  449.1 179.7 all-reduce.4

commit v2 on v0

--- a/solution.py
+++ b/solution.py
@@ -6,6 +6,12 @@
 
 HALO = 128
 highest = lax.Precision.HIGHEST
+
+
+def summed_here(x, axis):
+    parts = lax.all_gather(x, axis, axis=0, tiled=False)
+    summed = parts.sum(axis=0)
+    return summed
 
 
 def extended_2(block, sides, width):
@@ -48,7 +54,7 @@
 
 
 def gram_over_space(partial_value):
-    return lax.psum(partial_value, "space")
+    return summed_here(partial_value, "space")
 
 
 def orthonormal(rows, reduce_gram):

time: 698 us -> 472 us (0.68)
  waiting for transfers between devices: 431 us -> 205 us
    psum x2 -> x0, waiting for transfers between devices: 367 us -> none  [gram_over_space(): return lax.psum(partial_value, 'space')]
    all_gather x0 -> x2, waiting for transfers between devices: none -> 141 us  [summed_here(): parts = lax.all_gather(x, axis, axis=0, tiled=False)]
  transfers between devices with their start and end apart: 7 -> 7, of which waited for: 4 -> 4; matrix products, arithmetic and copies ran while one was open for 1% -> 2% of each run, Pallas kernels for 0% -> 0%
where the time goes in v2:
time: 472 us
  waiting for transfers between devices  205 us (43%)
  other arithmetic  142 us (30%)
  local copies, waits for them, and re-layouts  79.9 us (17%)
  starting transfers between devices  15.9 us (3%)
  matrix products  14.6 us (3%)
  between operations  14.1 us (3%)
    all_gather x2, waiting for transfers between devices, summed_here(): parts = lax.all_gather(x, axis, axis=0, tiled=False)  141 us
    scatter-add x1, other arithmetic, element_images(): return jnp.zeros(extended.shape, jnp.float32).at[:, local].add(pulled)  88.2 us
    all_gather x1, waiting for transfers between devices, on_device(): whole = lax.all_gather(images, 'probe', axis=0, tiled=True)  62.5 us
    gather x2, local copies, waits for them, and re-layouts, element_images(): gathered = extended[:, local]  60.3 us
    another operation x3, other arithmetic, orthonormal(): lower_second = jnp.linalg.cholesky(gram_second)  12.6 us
    another operation x3, other arithmetic, orthonormal(): lower_first = jnp.linalg.cholesky(gram_first)  12.4 us
    another operation x2, other arithmetic, orthonormal(): lax.linalg.triangular_solve(lower_first, rows, left_side=True, lower=True)  10.5 us
    another operation x2, other arithmetic, orthonormal(): lax.linalg.triangular_solve(lower_second, basis_first, left_side=True, lo...  10.4 us
  transfers between devices with their start and end apart: 7, of which 4 were waited for; matrix products, arithmetic and copies ran while one was open for 2% of the time, Pallas kernels for 0%

profile of v2, /device:TPU:1, one launch (start us, length us, event | category | flops | bytes accessed | tf_op | source)
XLA Modules:
  0.0 471.5 jit_solution(9732390869500762336)
XLA Ops:
  7.9 4.9 %collective-permute-start = (f32[8,128]{1,0:T(8,128)S(1)}, f32[8,128]{1,0:T(8,128)S(1)}, u32[]{:S(2)}, u32[]{:S(2)}) collective-permute-start(f32[8,128]{1,0:T(8,128)S(1)} %get-tuple-element.103), channel_id=1, source_target_pairs={{0,1},{1,2},{2,3},{3,4},{4,5},{5,6},{6,7},{7,8},{8,9},{9,10},{10,1... | collective-permute-start | bytes 12296 | tf_op jit(solution)/shard_map/ppermute | solution.py:22
  12.8 5.1 %collective-permute-start.1 = (f32[8,128]{1,0:T(8,128)S(1)}, f32[8,128]{1,0:T(8,128)S(1)}, u32[]{:S(2)}, u32[]{:S(2)}) collective-permute-start(f32[8,128]{1,0:T(8,128)S(1)} %get-tuple-element.104), channel_id=1, source_target_pairs={{1,0},{2,1},{3,2},{4,3},{5,4},{6,5},{7,6},{8,7},{9,8},{10,9},{11,1... | collective-permute-start | bytes 12296 | tf_op jit(solution)/shard_map/ppermute | solution.py:25
  18.0 1.7 fusion.28
  21.4 1.9 fusion.26
  28.8 54.8 %gather_fusion = f32[16384,8]{1,0:T(8,128)} fusion(f32[8,4352]{0,1:T(8,128)S(1)} %copy.37, s32[16384]{0:T(1024)S(1)} %broadcast_clamp_fusion), kind=kCustom, calls=%fused_computation | custom fusion | bytes 1114112 | tf_op jit(solution)/shard_map/gather | solution.py:37
  83.6 5.5 %copy.38 = f32[16384,8]{0,1:T(8,128)S(1)} copy(f32[16384,8]{1,0:T(8,128)} %gather_fusion) | data formatting | bytes 1048576 | tf_op jit(solution)/shard_map/gather | solution.py:37
  91.7 4.6 copy.53
  96.3 88.2 %scatter_custom_fusion = f32[8,4352]{0,1:T(8,128)S(1)} fusion(s32[16384]{0:T(1024)S(1)} %bitcast.112, f32[16384,8]{1,0:T(8,128)} %bitcast.106, f32[]{:T(128)} %constant.96.clone.1), kind=kCustom, calls=%fused_computation.3 | custom fusion | flops 131072 | bytes 139776 | tf_op jit(solution)/shard_map/scatter-add | solution.py:53
  185.9 2.2 copy.54
  188.2 1.9 collective-permute-start.2
  190.2 3.7 collective-permute-start.3
  195.9 62.5 %all-gather.6.cloned.1.call-done = f32[128,4096]{1,0:T(8,128)} async-done(((f32[8,4096]{1,0:T(8,128)}), f32[128,4096]{1,0:T(8,128)}) %all-gather.6.cloned.1.call-update) | async-done | bytes 2097168 | tf_op jit(solution)/shard_map/all_gather | solution.py:88
  258.5 4.7 fusion.32
  263.4 72.8 %all-gather.8.cloned.1.call-done = f32[4096,128]{1,0:T(8,128)} async-done(((f32[128,128]{1,0:T(8,128)}), f32[4096,128]{1,0:T(8,128)}) %all-gather.8.cloned.1.call-update) | async-done | bytes 2097168 | tf_op jit(solution)/shard_map/all_gather | solution.py:12
  336.2 1.7 reduce_sum.18
  338.0 11.7 %cholesky.44 = f32[128,128]{1,0:T(8,128)S(1)} custom-call(f32[128,128]{1,0:T(8,128)S(1)} %fusion.8), custom_call_target="Cholesky" | custom-call | tf_op jit(solution)/shard_map/jit(cholesky)/cholesky | solution.py:64
  351.1 9.8 %custom-call.6 = f32[1,128,128]{1,2,0:T(8,128)S(1)} custom-call(f32[1,128,128]{2,1,0:T(8,128)S(1)} %fusion.12), custom_call_target="InvertDiagBlocksLowerTriangular" | custom-call | tf_op jit(solution)/shard_map/triangular_solve/custom-call.0 | solution.py:65
  360.9 3.5 fusion.6
  364.4 2.4 fusion.33
  366.8 68.6 %all-gather.10.cloned.1.call-done = f32[4096,128]{1,0:T(8,128)} async-done(((f32[128,128]{1,0:T(8,128)}), f32[4096,128]{1,0:T(8,128)}) %all-gather.10.cloned.1.call-update) | async-done | bytes 2097168 | tf_op jit(solution)/shard_map/all_gather | solution.py:12
  437.2 11.9 %cholesky.55 = f32[128,128]{1,0:T(8,128)S(1)} custom-call(f32[128,128]{1,0:T(8,128)S(1)} %fusion.5), custom_call_target="Cholesky" | custom-call | tf_op jit(solution)/shard_map/jit(cholesky)/cholesky | solution.py:69
  449.8 2.1 convolution_multiply_fusion
  452.5 9.8 %custom-call.7 = f32[1,128,128]{1,2,0:T(8,128)S(1)} custom-call(f32[1,128,128]{2,1,0:T(8,128)S(1)} %select_bitcast_fusion), custom_call_target="InvertDiagBlocksLowerTriangular" | custom-call | tf_op jit(solution)/shard_map/triangular_solve/custom-call.0 | solution.py:70
  462.4 1.9 fusion.3
  (62 shorter events, 19.5 us)
Async XLA Ops:
  7.2 251.3 %all-gather.6.cloned.1.call-start = ((), (), s32[]{:S(2)}) async-start(), calls=%async_computation | async-start | bytes 2228224 | tf_op jit(solution)/shard_map/all_gather | solution.py:88
  7.9 19.3 %collective-permute-start = (f32[8,128]{1,0:T(8,128)S(1)}, f32[8,128]{1,0:T(8,128)S(1)}, u32[]{:S(2)}, u32[]{:S(2)}) collective-permute-start(f32[8,128]{1,0:T(8,128)S(1)} %get-tuple-element.103), channel_id=1, source_target_pairs={{0,1},{1,2},{2,3},{3,4},{4,5},{5,6},{6,7},{7,8},{8,9},{9,10},{10,1... | collective-permute-start | bytes 12296 | tf_op jit(solution)/shard_map/ppermute | solution.py:22
  12.8 14.4 %collective-permute-start.1 = (f32[8,128]{1,0:T(8,128)S(1)}, f32[8,128]{1,0:T(8,128)S(1)}, u32[]{:S(2)}, u32[]{:S(2)}) collective-permute-start(f32[8,128]{1,0:T(8,128)S(1)} %get-tuple-element.104), channel_id=1, source_target_pairs={{1,0},{2,1},{3,2},{4,3},{5,4},{6,5},{7,6},{8,7},{9,8},{10,9},{11,1... | collective-permute-start | bytes 12296 | tf_op jit(solution)/shard_map/ppermute | solution.py:25
  185.9 7.9 %copy-start = (f32[8,4096]{1,0:T(8,128)S(1)}, f32[8,4096]{1,0:T(8,128)}, u32[]{:S(2)}) copy-start(f32[8,4096]{1,0:T(8,128)} %param.12) | copy-start | bytes 393220
  185.9 7.9 %copy-start.2 = (f32[4096]{0:T(1024)S(1)}, f32[4096]{0:T(1024)}, u32[]{:S(2)}) copy-start(f32[4096]{0:T(1024)} %param.15) | copy-start | bytes 49156
  188.2 5.7 %collective-permute-start.2 = (f32[8,128]{1,0:T(8,128)S(1)}, f32[8,128]{1,0:T(8,128)S(1)}, u32[]{:S(2)}, u32[]{:S(2)}) collective-permute-start(f32[8,128]{1,0:T(8,128)S(1)} %copy.55), channel_id=1, source_target_pairs={{1,0},{2,1},{3,2},{4,3},{5,4},{6,5},{7,6},{8,7},{9,8},{10,9},{11,1... | collective-permute-start | bytes 12296 | tf_op jit(solution)/shard_map/ppermute | solution.py:33
  190.2 4.4 collective-permute-start.3
  195.2 0.7 copy-start.1
  195.9 140.3 %all-gather.8.cloned.1.call-start = ((), (), s32[]{:S(2)}) async-start(), calls=%async_computation.1 | async-start | bytes 2162688 | tf_op jit(solution)/shard_map/all_gather | solution.py:12
  263.2 172.2 %all-gather.10.cloned.1.call-start = ((), (), s32[]{:S(2)}) async-start(), calls=%async_computation.2 | async-start | bytes 2162688 | tf_op jit(solution)/shard_map/all_gather | solution.py:12
Sparse Core Ops, SparseCore 0:
  196.0 62.4 all-gather.5
  263.3 72.8 all-gather.7
  366.9 68.4 all-gather.9
